TPU v7x, 32 devices: a whole 2x2x4 slice. The times are simulated.
32 devices in a mesh: dp: 8 (over z, x), seq: 4 (over y, core).
Axes of the slice: x: 2, y: 2, z: 4, core: 2. Of those that a mesh axis runs over, the one named last changes fastest.
Arguments:
- tokens: bfloat16 [8, 1024, 1600], P('dp', 'seq'), may hold values from -6 to 6
- cotangent: bfloat16 [8, 1024, 1600], P('dp', 'seq'), may hold values from -6 to 6
- lengths: int32 [8], P('dp'), may hold values from 256 to 1024, as said below
- w_qkv: bfloat16 [7680000], P(('dp', 'seq')), may hold values from -0.15625 to 0.15625
- w_out: bfloat16 [2560000], P(('dp', 'seq')), may hold values from -2.5 to 2.5
- w_fc: bfloat16 [10246400], P(('dp', 'seq')), may hold values from -0.15625 to 0.15625
- w_proj: bfloat16 [10240000], P(('dp', 'seq')), may hold values from -0.078125 to 0.078125
- attention_vectors: bfloat16 [6400], P(('dp', 'seq')), as said below
- block_vectors: bfloat16 [6400], P(('dp', 'seq')), as said below
Outputs:
- output: bfloat16 [8, 1024, 1600], P('dp', 'seq')
- input_grad: float32 [8, 1024, 1600], P('dp', 'seq')
- grad_qkv: float32 [7680000], P(('dp', 'seq'))
- grad_out: float32 [2560000], P(('dp', 'seq'))
- grad_fc: float32 [10246400], P(('dp', 'seq'))
- grad_proj: float32 [10240000], P(('dp', 'seq'))
- grad_attention_vectors: float32 [6400], P(('dp', 'seq'))
- grad_block_vectors: float32 [6400], P(('dp', 'seq'))
Inputs may be any that keep to these rules, and one draw needn't show every extreme that they name: `lengths`: valid positions of each slot; in every draw one slot has all 1024 and one has 256. `attention_vectors`: gains near one, biases of order one half. `block_vectors`: gains near one, biases of order one half.
All inputs are finite; a program needn't handle non-finite values.
Results may differ from a plain program's by a relative error of at most 0.01.
Values may be sent and summed in bfloat16 or wider, within the bound.
No kernel may reach another device: no remote copies, remote signals or barrier semaphores. Data moves between devices by JAX's collectives and lax.ppermute only.
A program may use at most 448 MiB of HBM per device.

v0:
```python
from functools import partial
import jax
import jax.numpy as jnp
from jax import lax
from jax.sharding import PartitionSpec as P

HD = 64
EPS = 1e-05


def layer_norm(value, gain, shift):
    centre = value - jnp.mean(value, axis=-1, keepdims=True)
    spread = jnp.mean(centre * centre, axis=-1, keepdims=True)
    return centre * lax.rsqrt(spread + EPS) * gain + shift


def tanh_gelu(value):
    return jax.nn.gelu(value, approximate=True)


def split_weights(gathered, width):
    flat_qkv, flat_out, flat_fc, flat_proj, first_vectors, second_vectors = gathered
    hidden = flat_fc.shape[0] // (width + 1)
    expand_full = flat_fc.reshape(width + 1, hidden)
    token_rows = (
        jnp.concatenate([first_vectors, second_vectors]).astype(jnp.float32).reshape(8, width)
    )
    expand_bias = expand_full[width].astype(jnp.float32)
    return (
        flat_qkv.reshape(width, 3 * width),
        flat_out.reshape(width, width),
        expand_full[:width],
        flat_proj.reshape(hidden, width),
        token_rows,
        expand_bias,
    )


def to_heads(value, heads):
    slots, count, width = value.shape
    return jnp.moveaxis(value.reshape(slots, count, heads, width // heads), 2, 0)


def from_heads(value):
    heads, slots, count, size = value.shape
    return jnp.moveaxis(value, 0, 2).reshape(slots, count, heads * size)


def head_scores(allowed, query, keys):
    scores = jnp.einsum("sqd,skd->sqk", query, keys, preferred_element_type=jnp.float32) * 0.125
    return jnp.where(allowed, scores, -1e30)


def head_forward(allowed, item):
    query, keys, values = item
    scores = head_scores(allowed, query, keys)
    peak = jnp.max(scores, axis=-1, keepdims=True)
    raised = jnp.exp(scores - peak)
    total = jnp.sum(raised, axis=-1, keepdims=True)
    weights = (raised / total).astype(jnp.bfloat16)
    result = jnp.einsum("sqk,skd->sqd", weights, values, preferred_element_type=jnp.float32)
    return (result, (peak + jnp.log(total))[..., 0])


def head_backward(allowed, item):
    query, keys, values, grad_result, normal = item
    scores = head_scores(allowed, query, keys)
    probs = jnp.where(allowed, jnp.exp(scores - normal[..., None]), 0.0)
    weights = probs.astype(jnp.bfloat16)
    grad_probs = jnp.einsum("sqd,skd->sqk", grad_result, values, preferred_element_type=jnp.float32)
    inner_total = jnp.sum(probs * grad_probs, axis=-1, keepdims=True)
    grad_scores = (probs * (grad_probs - inner_total) * 0.125).astype(jnp.bfloat16)
    grad_query = jnp.einsum("sqk,skd->sqd", grad_scores, keys, preferred_element_type=jnp.float32)
    grad_keys = jnp.einsum("sqk,sqd->skd", grad_scores, query, preferred_element_type=jnp.float32)
    grad_values = jnp.einsum(
        "sqk,sqd->skd", weights, grad_result, preferred_element_type=jnp.float32
    )
    return (grad_query, grad_keys, grad_values)


def local(tokens, cotangent, lengths, w_qkv, w_out, w_fc, w_proj, attention_vectors, block_vectors):
    slots, count, width = tokens.shape
    heads = width // HD
    rank = lax.axis_index("seq")
    span = count * lax.axis_size("seq")
    part_qkv, part_out, part_fc, part_proj, part_first, part_second = (
        lax.all_gather(w_qkv, "seq", axis=0, tiled=True),
        lax.all_gather(w_out, "seq", axis=0, tiled=True),
        lax.all_gather(w_fc, "seq", axis=0, tiled=True),
        lax.all_gather(w_proj, "seq", axis=0, tiled=True),
        lax.all_gather(attention_vectors, "seq", axis=0, tiled=True),
        lax.all_gather(block_vectors, "seq", axis=0, tiled=True),
    )
    gathered = (
        lax.all_gather(part_qkv, "dp", axis=0, tiled=True),
        lax.all_gather(part_out, "dp", axis=0, tiled=True),
        lax.all_gather(part_fc, "dp", axis=0, tiled=True),
        lax.all_gather(part_proj, "dp", axis=0, tiled=True),
        lax.all_gather(part_first, "dp", axis=0, tiled=True),
        lax.all_gather(part_second, "dp", axis=0, tiled=True),
    )
    (
        query_key_value_weight,
        output_weight,
        expand_weight,
        contract_weight,
        token_rows,
        expand_bias,
    ) = split_weights(gathered, width)
    place = rank * count + jnp.arange(count)
    key_place = jnp.arange(span)
    allowed = (key_place[None, None, :] <= place[None, :, None]) & (
        key_place[None, None, :] < lengths[:, None, None]
    )
    valid = place[None, :] < lengths[:, None]
    source = tokens.astype(jnp.float32)
    normed_low = layer_norm(source, token_rows[0], token_rows[1]).astype(jnp.bfloat16)
    mixed_heads = jnp.einsum(
        "scd,de->sce", normed_low, query_key_value_weight, preferred_element_type=jnp.float32
    )
    query = (mixed_heads[..., :width] + token_rows[2]).astype(jnp.bfloat16)
    keys = mixed_heads[..., width : 2 * width].astype(jnp.bfloat16)
    values = (mixed_heads[..., 2 * width :] + token_rows[3]).astype(jnp.bfloat16)
    all_keys, all_values = (
        lax.all_gather(keys, "seq", axis=1, tiled=True),
        lax.all_gather(values, "seq", axis=1, tiled=True),
    )
    query_heads = to_heads(query, heads)
    key_heads = to_heads(all_keys, heads)
    value_heads = to_heads(all_values, heads)
    head_result, normal = lax.map(
        partial(head_forward, allowed), (query_heads, key_heads, value_heads)
    )
    attention_output = from_heads(head_result).astype(jnp.bfloat16)
    middle_state = (
        source
        + jnp.einsum(
            "scd,de->sce", attention_output, output_weight, preferred_element_type=jnp.float32
        )
        + token_rows[4]
    )
    second_normed = layer_norm(middle_state, token_rows[5], token_rows[6]).astype(jnp.bfloat16)
    inner_hidden = (
        jnp.einsum("scd,df->scf", second_normed, expand_weight, preferred_element_type=jnp.float32)
        + expand_bias
    )
    active_low = tanh_gelu(inner_hidden).astype(jnp.bfloat16)
    result = (
        middle_state
        + jnp.einsum("scf,fd->scd", active_low, contract_weight, preferred_element_type=jnp.float32)
        + token_rows[7]
    )
    output = result.astype(jnp.bfloat16)
    again_qkv, again_out, again_fc, again_proj, again_first, again_second = (
        lax.all_gather(w_qkv, "seq", axis=0, tiled=True),
        lax.all_gather(w_out, "seq", axis=0, tiled=True),
        lax.all_gather(w_fc, "seq", axis=0, tiled=True),
        lax.all_gather(w_proj, "seq", axis=0, tiled=True),
        lax.all_gather(attention_vectors, "seq", axis=0, tiled=True),
        lax.all_gather(block_vectors, "seq", axis=0, tiled=True),
    )
    again = (
        lax.all_gather(again_qkv, "dp", axis=0, tiled=True),
        lax.all_gather(again_out, "dp", axis=0, tiled=True),
        lax.all_gather(again_fc, "dp", axis=0, tiled=True),
        lax.all_gather(again_proj, "dp", axis=0, tiled=True),
        lax.all_gather(again_first, "dp", axis=0, tiled=True),
        lax.all_gather(again_second, "dp", axis=0, tiled=True),
    )
    (
        query_key_value_weight,
        output_weight,
        expand_weight,
        contract_weight,
        token_rows,
        expand_bias,
    ) = split_weights(again, width)
    grad_result = cotangent * valid.astype(jnp.bfloat16)[..., None]
    grad_wide = grad_result.astype(jnp.float32)
    grad_proj = jnp.einsum(
        "scf,scd->fd", active_low, grad_result, preferred_element_type=jnp.float32
    )
    bias_proj_grad = jnp.sum(grad_wide, axis=(0, 1))
    grad_active = jnp.einsum(
        "scd,fd->scf", grad_result, contract_weight, preferred_element_type=jnp.float32
    )
    gelu_back = jax.vjp(tanh_gelu, inner_hidden)[1]
    inner_low = gelu_back(grad_active)[0].astype(jnp.bfloat16)
    bias_fc_grad = jnp.sum(inner_low.astype(jnp.float32), axis=(0, 1))
    grad_fc = jnp.einsum(
        "scd,scf->df", second_normed, inner_low, preferred_element_type=jnp.float32
    )
    grad_fc_full = jnp.concatenate([grad_fc, bias_fc_grad[None, :]], axis=0).reshape(-1)
    grad_normed_two = jnp.einsum(
        "scf,df->scd", inner_low, expand_weight, preferred_element_type=jnp.float32
    )
    norm_two_back = jax.vjp(layer_norm, middle_state, token_rows[5], token_rows[6])[1]
    grad_mid, gain_two_grad, shift_two_grad = norm_two_back(grad_normed_two)
    grad_mid = grad_mid + grad_wide
    branch_low = grad_mid.astype(jnp.bfloat16)
    bias_out_grad = jnp.sum(branch_low.astype(jnp.float32), axis=(0, 1))
    grad_out_mat = jnp.einsum(
        "scd,sce->de", attention_output, branch_low, preferred_element_type=jnp.float32
    )
    grad_attended = jnp.einsum(
        "sce,de->scd", branch_low, output_weight, preferred_element_type=jnp.float32
    ).astype(jnp.bfloat16)
    grad_query, grad_keys, grad_values = lax.map(
        partial(head_backward, allowed),
        (query_heads, key_heads, value_heads, to_heads(grad_attended, heads), normal),
    )
    keys_sum, values_sum = (
        lax.psum_scatter(from_heads(grad_keys), "seq", scatter_dimension=1, tiled=True),
        lax.psum_scatter(from_heads(grad_values), "seq", scatter_dimension=1, tiled=True),
    )
    query_low = from_heads(grad_query).astype(jnp.bfloat16)
    keys_low = keys_sum.astype(jnp.bfloat16)
    values_low = values_sum.astype(jnp.bfloat16)
    bias_query_grad = jnp.sum(query_low.astype(jnp.float32), axis=(0, 1))
    bias_value_grad = jnp.sum(values_low.astype(jnp.float32), axis=(0, 1))
    grad_mixed = jnp.concatenate([query_low, keys_low, values_low], axis=-1)
    grad_qkv = jnp.einsum("scd,sce->de", normed_low, grad_mixed, preferred_element_type=jnp.float32)
    grad_normed = jnp.einsum(
        "sce,de->scd", grad_mixed, query_key_value_weight, preferred_element_type=jnp.float32
    )
    norm_one_back = jax.vjp(layer_norm, source, token_rows[0], token_rows[1])[1]
    grad_source, gain_one_grad, shift_one_grad = norm_one_back(grad_normed)
    input_grad = grad_mid + grad_source
    first_grad = jnp.concatenate([gain_one_grad, shift_one_grad, bias_query_grad, bias_value_grad])
    second_grad = jnp.concatenate([bias_out_grad, gain_two_grad, shift_two_grad, bias_proj_grad])
    qkv_part, out_part, fc_part, proj_part, first_part, second_part = (
        lax.psum_scatter(grad_qkv.reshape(-1), "dp", scatter_dimension=0, tiled=True),
        lax.psum_scatter(grad_out_mat.reshape(-1), "dp", scatter_dimension=0, tiled=True),
        lax.psum_scatter(grad_fc_full, "dp", scatter_dimension=0, tiled=True),
        lax.psum_scatter(grad_proj.reshape(-1), "dp", scatter_dimension=0, tiled=True),
        lax.psum_scatter(first_grad, "dp", scatter_dimension=0, tiled=True),
        lax.psum_scatter(second_grad, "dp", scatter_dimension=0, tiled=True),
    )
    qkv_shard, out_shard, fc_shard, proj_shard, first_shard, second_shard = (
        lax.psum_scatter(qkv_part, "seq", scatter_dimension=0, tiled=True),
        lax.psum_scatter(out_part, "seq", scatter_dimension=0, tiled=True),
        lax.psum_scatter(fc_part, "seq", scatter_dimension=0, tiled=True),
        lax.psum_scatter(proj_part, "seq", scatter_dimension=0, tiled=True),
        lax.psum_scatter(first_part, "seq", scatter_dimension=0, tiled=True),
        lax.psum_scatter(second_part, "seq", scatter_dimension=0, tiled=True),
    )
    return (
        output,
        input_grad,
        qkv_shard,
        out_shard,
        fc_shard,
        proj_shard,
        first_shard,
        second_shard,
    )


def solution(mesh):
    in_specs = (
        P("dp", "seq", None),
        P("dp", "seq", None),
        P("dp"),
        P(("dp", "seq")),
        P(("dp", "seq")),
        P(("dp", "seq")),
        P(("dp", "seq")),
        P(("dp", "seq")),
        P(("dp", "seq")),
    )
    out_specs = (
        P("dp", "seq", None),
        P("dp", "seq", None),
        P(("dp", "seq")),
        P(("dp", "seq")),
        P(("dp", "seq")),
        P(("dp", "seq")),
        P(("dp", "seq")),
        P(("dp", "seq")),
    )
    return jax.shard_map(local, mesh=mesh, in_specs=in_specs, out_specs=out_specs, check_vma=False)
```

profile of v0, /device:TPU:0, one launch (start us, length us, event | category | flops | bytes accessed | tf_op | source)
XLA Modules:
  0.0 6387.4 jit_solution(10073918586808207974)
XLA Ops:
  7.2 6.3 reshape.576
  15.8 5.9 dynamic-update-slice.4
  23.4 25.4 all-gather.19.cloned.1.call-done
  49.0 8.1 reshape.584
  57.3 19.0 all-gather.2
  77.1 40.4 all-reduce.29.cloned.1.call-done
  117.4 7.4 broadcast.247
  124.8 39.2 dynamic-update-slice.5
  166.0 6.0 all-reduce.23
  172.5 51.9 all-reduce.22
  226.2 478.7 %all-gather.21.cloned.1.call-done = bf16[8,1,960000]{2,1,0:T(2,128)(2,1)} async-done(((bf16[1,1,960000]{2,1,0:T(2,128)(2,1)}), bf16[8,1,960000]{2,1,0:T(2,128)(2,1)}) %all-gather.21.cloned.1.call-update) | async-done | bytes 15360016 | tf_op jit(solution)/shard_map/all_gather | solution.py:95
  704.9 325.4 %reduce.24 = bf16[8,960000]{1,0:T(8,128)(2,1)} reduce(bf16[8,1,960000]{2,1,0:T(2,128)(2,1)} %all-gather.21.cloned.1.call-done, bf16[]{:T(256)} %constant.172), dimensions={1}, to_apply=%all-gather.1.reduce_sub_computation | reduce | bytes 30720002 | tf_op jit(solution)/shard_map/all_gather | solution.py:95
  1030.3 34.2 reshape.626
  1064.5 25.2 reshape.541
  1089.7 14.8 convolution_bitcast_fusion.4
  1110.4 17.7 reduce.26
  1133.1 32.0 reduce.25
  1165.2 12.3 reshape.628
  1177.5 9.6 reshape.545
  1187.1 325.9 %all-reduce.31.cloned.1.call-done = bf16[10246400]{0:T(1024)(128)(2,1)} async-done(((bf16[10246400]{0:T(1024)(128)(2,1)}), bf16[10246400]{0:T(1024)(128)(2,1)}) %all-reduce.31.cloned.1.call-update) | async-done | bytes 20492816
  1513.1 16.9 slice.87
  1530.0 35.4 slice.74
  1568.0 7.0 copy.27
  1576.0 7.1 copy.28
  1583.3 79.7 %while.28 = (s32[]{:T(128)}, bf16[25,1,256,64]{2,3,1,0:T(8,128)(2,1)S(1)}, f32[25,1,256]{2,1,0:T(1,128)S(1)}, bf16[25,1,256,64]{3,2,1,0:T(8,128)(2,1)}, bf16[25,...) while((s32[]{:T(128)}, ...), condition=%wide.region_5.6_spmd.clone, body=%wide.region_2.5_spmd.clone.sunk | while | flops 69730048 | bytes 3815529 | solution.py:131
  1663.0 5.3 fusion.110
  1668.6 12.4 convolution_add_fusion
  1681.0 289.2 %all-gather.17.cloned.1.call-done = bf16[10240000]{0:T(1024)(128)(2,1)} async-done(((bf16[1280000]{0:T(1024)(128)(2,1)}), bf16[10240000]{0:T(1024)(128)(2,1)}) %all-gather.17.cloned.1.call-update) | async-done | bytes 20480016 | tf_op jit(solution)/shard_map/all_gather | solution.py:98
  1970.3 34.0 reshape.547
  2004.2 14.1 convert_reduce_fusion
  2018.3 13.4 fusion.74
  2039.8 200.8 %while.29 = (s32[]{:T(128)}, bf16[25,1,256,64]{2,3,1,0:T(8,128)(2,1)S(1)}, f32[25,1,1024,64]{2,3,1,0:T(8,128)}, f32[25,1,1024,64]{2,3,1,0:T(8,128)}, bf16[25,1,2...) while((s32[]{:T(128)}, ...), condition=%wide.region_12.13_spmd.clone, body=%wide.region_10.12_spmd.clone.sunk | while | flops 171179776 | bytes 9515137 | solution.py:208
  2241.4 22.7 fusion.84
  2264.1 48.3 reshape.557
  2312.4 7.0 fusion.81
  2319.4 13.5 reshape.555
  2332.8 18.4 fusion.101
  2351.2 28.1 pad_maximum_fusion
  2379.3 39.9 reshape.556
  2424.4 13.8 fusion.77
  2438.2 36.5 reshape.554
  2477.1 3609.6 %all-reduce.33.cloned.1.call-done = (f32[7680000]{0:T(1024)}, f32[2560000]{0:T(1024)}, f32[10246400]{0:T(1024)}, f32[10240000]{0:T(1024)}) async-done(((f32[7680000]{0:T(1024)}, f32[2560000]{0:T(1024)}, f32[10246400]{0:T(1024)}, f32[10240000]{0:T(1024)}), (f32[7680000]{0:T(1024)}, f32[2560000]{0:T(1024)}, f32[10246400]{0:T(1024)}, f32[10240000]{0:T(1024)})) %all-reduce.33.cloned.1.call-update) | async-done | bytes 122905616
  6086.8 5.1 dynamic-slice.7
  6110.5 17.3 fusion.60
  6127.8 8.2 fusion.71
  6137.3 35.6 all-reduce.18
  6173.1 6.4 all-reduce.20
  6184.1 186.5 %all-reduce.35.cloned.1.call-done = (f32[960000]{0:T(1024)}, f32[320000]{0:T(1024)}, f32[1280800]{0:T(1024)}, f32[1280000]{0:T(1024)}) async-done(((f32[960000]{0:T(1024)}, f32[320000]{0:T(1024)}, f32[1280800]{0:T(1024)}, f32[1280000]{0:T(1024)}), (f32[960000]{0:T(1024)}, f32[320000]{0:T(1024)}, f32[1280800]{0:T(1024)}, f32[1280000]{0:T(1024)})) %all-reduce.35.cloned.1.call-update) | async-done | bytes 15363216
  (465 shorter events, 344.2 us)
Async XLA Ops:
  7.2 8.7 copy-start.12
  7.2 41.7 all-gather.19.cloned.1.call-start
  13.5 103.9 %all-reduce.29.cloned.1.call-start = ((), (), s32[]{:S(2)}) async-start(), calls=%async_computation.7 | async-start | bytes 5124096
  21.7 1.6 copy-start.3
  21.7 27.2 copy-start.13
  23.4 681.5 %all-gather.21.cloned.1.call-start = ((), (), s32[]{:S(2)}) async-start(), calls=%async_computation.10 | async-start | bytes 34560000 | tf_op jit(solution)/shard_map/all_gather | solution.py:95
  48.9 8.2 copy-start.16
  48.9 1061.5 %all-gather.25.cloned.1.call-start = ((), (), s32[]{:S(2)}) async-start(), calls=%async_computation.12 | async-start | bytes 6400000 | tf_op jit(solution)/shard_map/all_gather | solution.py:90
  57.1 1076.1 %all-gather.23.cloned.1.call-start = ((), (), s32[]{:S(2)}) async-start(), calls=%async_computation.11 | async-start | bytes 11520000 | tf_op jit(solution)/shard_map/all_gather | solution.py:96
  76.4 1436.7 %all-reduce.31.cloned.1.call-start = ((), (), s32[]{:S(2)}) async-start(), calls=%async_computation.8 | async-start | bytes 40988672
  117.4 7.4 copy-start.11
  164.0 1.5 copy-start.33
  164.0 1.7 copy-start.34
  164.0 60.4 copy-start
  164.0 1403.9 %all-gather.13.cloned.1.call-start = ((), (), s32[]{:S(2)}) async-start(), calls=%async_computation.2 | async-start | bytes 4096000 | tf_op jit(solution)/shard_map/all_gather | solution.py:125
  224.6 865.1 %copy-start.19 = (f32[256]{0:T(256)}, f32[256]{0:T(256)S(1)}, u32[]{:S(2)}) copy-start(f32[256]{0:T(256)S(1)} %broadcast_multiply_fusion.1) | copy-start | bytes 3076
  224.9 0.6 copy-start.27
  224.9 864.8 %copy-start.21 = (f32[256]{0:T(256)}, f32[256]{0:T(256)S(1)}, u32[]{:S(2)}) copy-start(f32[256]{0:T(256)S(1)} %fusion.95) | copy-start | bytes 3076
  226.2 863.5 %copy-start.14 = (f32[1600]{0:T(1024)}, f32[1600]{0:T(1024)S(1)}, u32[]{:S(2)}) copy-start(f32[1600]{0:T(1024)S(1)} %get-tuple-element.229) | copy-start | bytes 19204
  226.2 863.6 %copy-start.17 = (f32[1600]{0:T(1024)}, f32[1600]{0:T(1024)S(1)}, u32[]{:S(2)}) copy-start(f32[1600]{0:T(1024)S(1)} %get-tuple-element.228) | copy-start | bytes 19204
  1107.0 469.1 %all-gather.15.cloned.1.call-start = ((), (), s32[]{:S(2)}) async-start(), calls=%async_computation.3 | async-start | bytes 4096000 | tf_op jit(solution)/shard_map/all_gather | solution.py:126
  1110.4 859.9 %all-gather.17.cloned.1.call-start = ((), (), s32[]{:S(2)}) async-start(), calls=%async_computation.4 | async-start | bytes 23040000 | tf_op jit(solution)/shard_map/all_gather | solution.py:98
  1132.3 1286.9 %reduce-scatter.3.cloned.1.call-start = ((), (), s32[]{:S(2)}) async-start(), calls=%async_computation.5 | async-start | bytes 8192000 | tf_op jit(solution)/shard_map/reduce_scatter | solution.py:213
  1133.1 1108.3 %copy-start.31 = (bf16[256]{0:T(256)(128)(2,1)}, bf16[256]{0:T(256)(128)(2,1)S(1)}, u32[]{:S(2)}) copy-start(bf16[256]{0:T(256)(128)(2,1)S(1)} %compare_convert_fusion) | copy-start | bytes 1540
  1663.0 5.3 copy-start.7
  1681.0 323.2 %copy-start.4 = (bf16[1,256,1600]{1,2,0:T(8,128)(2,1)S(1)}, bf16[1,256,1600]{1,2,0:T(8,128)(2,1)}, u32[]{:S(2)}) copy-start(bf16[1,256,1600]{1,2,0:T(8,128)(2,1)} %param.14) | copy-start | bytes 2457604
  2031.7 1.7 copy-start.6
  2032.2 5.7 copy-start.2
  2032.2 5.7 copy-start.25
  2033.5 4.5 copy-start.10
  2240.6 181.1 %reduce-scatter.5.cloned.1.call-start = ((), (), s32[]{:S(2)}) async-start(), calls=%async_computation.6 | async-start | bytes 8192000 | tf_op jit(solution)/shard_map/reduce_scatter | solution.py:214
  2241.3 3845.4 %all-reduce.33.cloned.1.call-start = ((), (), s32[]{:S(2)}) async-start(), calls=%async_computation.13 | async-start | bytes 245817344
  2264.1 48.3 copy-start.8
  2419.2 5.2 copy-start.1
  2419.2 5.2 copy-start.15
  2419.2 5.2 copy-start.18
  2419.2 5.2 copy-start.20
  2419.2 5.2 copy-start.22
  2423.5 0.9 copy-start.9
  2474.8 3895.8 %all-reduce.35.cloned.1.call-start = ((), (), s32[]{:S(2)}) async-start(), calls=%async_computation.14 | async-start | bytes 30736384
  6103.8 6.6 copy-start.23
  6103.8 6.6 copy-start.24
  6103.8 6.6 copy-start.30
  6103.8 6.7 copy-start.29
  6127.8 8.6 copy-start.28
  6136.0 44.8 copy-start.5
  6136.0 44.8 copy-start.26
  6136.1 44.7 copy-start.32
Sparse Core Ops, SparseCore 0:
  13.6 35.2 all-gather.18
  51.3 66.0 all-reduce.28
  119.0 585.7 all-gather.20
  706.9 39.7 all-gather.24
  749.0 147.8 all-gather.22
  901.4 611.6 all-reduce.30
  1515.3 28.8 all-gather.12
  1546.3 29.6 all-gather.14
  1577.7 392.5 all-gather.16
  2240.7 60.0 reduce-scatter.2
  2303.4 60.0 reduce-scatter.4
  2474.9 3611.7 all-reduce.32
  6103.9 266.6 all-reduce.34
where the time goes:
time: 6410 us; the launch traced here: 6390 us
  waiting for transfers between devices  4960 us (77%)
  other arithmetic  434 us (7%)
  local copies, waits for them, and re-layouts  433 us (7%)
  matrix products  418 us (7%)
  blocking collectives  119 us (2%)
    unnamed x17, waiting for transfers between devices  4160 us
    all_gather x1, waiting for transfers between devices, local(): lax.all_gather(part_qkv, 'dp', axis=0, tiled=True)  479 us
    all_gather x1, other arithmetic, local(): lax.all_gather(part_qkv, 'dp', axis=0, tiled=True)  325 us
    all_gather x1, waiting for transfers between devices, local(): lax.all_gather(part_proj, 'dp', axis=0, tiled=True)  289 us
    unnamed x101, local copies, waits for them, and re-layouts  152 us
  transfers between devices with their start and end apart: 13, of which 8 were waited for; matrix products, arithmetic and copies ran while one was open for 15% of the time, Pallas kernels for 0%

commit v1 on v0

--- a/solution.py
+++ b/solution.py
@@ -1,11 +1,35 @@
+import functools
 from functools import partial
 import jax
 import jax.numpy as jnp
 from jax import lax
 from jax.sharding import PartitionSpec as P
+from jax.lax import axis_index, axis_size, ppermute
 
 HD = 64
 EPS = 1e-05
+
+
+def _recast_patch(array_in, peer_axis):
+    left_arr = axis_size(peer_axis)
+    opened = axis_index(peer_axis)
+    piece_now, local_now = (left_arr, opened)
+    f_now, moved = (array_in, 1)
+    while moved < piece_now:
+        grid = []
+        b = 0
+        while b < piece_now:
+            grid.append((b, b ^ moved))
+            b += 1
+        m_next = ppermute(f_now, peer_axis, grid)
+        mixed_arr = jnp.concatenate([f_now, m_next], axis=0)
+        work_now = jnp.concatenate([m_next, f_now], axis=0)
+        f_now = jnp.where(local_now & moved == 0, mixed_arr, work_now)
+        moved = 2 * moved
+    return f_now
+
+
+switch_widths = functools.partial(_recast_patch, peer_axis="dp")
 
 
 def layer_norm(value, gain, shift):
@@ -92,7 +116,7 @@
         lax.all_gather(block_vectors, "seq", axis=0, tiled=True),
     )
     gathered = (
-        lax.all_gather(part_qkv, "dp", axis=0, tiled=True),
+        switch_widths(part_qkv),
         lax.all_gather(part_out, "dp", axis=0, tiled=True),
         lax.all_gather(part_fc, "dp", axis=0, tiled=True),
         lax.all_gather(part_proj, "dp", axis=0, tiled=True),

time: 6410 us -> 7070 us (1.10)
  blocking collectives: 119 us -> 516 us
  waiting for transfers between devices: 4960 us -> 5090 us
  other arithmetic: 434 us -> 515 us
    unnamed x4, blocking collectives: 100 us -> 497 us
    unnamed x17, waiting for transfers between devices: 4160 us -> 4060 us
    ppermute x0 -> x3, waiting for transfers between devices: none -> 104 us  [_recast_patch(): m_next = ppermute(f_now, peer_axis, grid)]
    all_gather x1, waiting for transfers between devices: 479 us -> 564 us  [local(): lax.all_gather(again_qkv, 'dp', axis=0, tiled=True)]
    all_gather x1 -> x2, other arithmetic: 325 us -> 362 us  [the longest x1 325 us: local(): lax.all_gather(again_qkv, 'dp', axis=0, tiled=True)]
    unnamed x101 -> x110, local copies, waits for them, and re-layouts: 152 us -> 159 us
  transfers between devices with their start and end apart: 13 -> 16, of which waited for: 8 -> 7; matrix products, arithmetic and copies ran while one was open for 15% -> 14% of each run, Pallas kernels for 0% -> 0%
where the time goes in v1:
time: 7070 us; the launch traced here: 7040 us
  waiting for transfers between devices  5090 us (72%)
  blocking collectives  516 us (7%)
  other arithmetic  515 us (7%)
  local copies, waits for them, and re-layouts  469 us (7%)
  matrix products  420 us (6%)
    unnamed x17, waiting for transfers between devices  4060 us
    all_gather x1, waiting for transfers between devices, local(): lax.all_gather(again_qkv, 'dp', axis=0, tiled=True)  564 us
    unnamed x4, blocking collectives  497 us
    all_gather x1, waiting for transfers between devices, local(): lax.all_gather(part_proj, 'dp', axis=0, tiled=True)  328 us
    all_gather x1, other arithmetic, local(): lax.all_gather(again_qkv, 'dp', axis=0, tiled=True)  325 us
    unnamed x110, local copies, waits for them, and re-layouts  159 us
  transfers between devices with their start and end apart: 16, of which 7 were waited for; matrix products, arithmetic and copies ran while one was open for 14% of the time, Pallas kernels for 0%

profile of v1, /device:TPU:0, one launch (start us, length us, event | category | flops | bytes accessed | tf_op | source)
XLA Modules:
  0.0 7040.6 jit_solution(6678895243366462060)
XLA Ops:
  13.5 35.3 all-gather.19.cloned.1.call-done
  48.8 37.1 reduce.24
  90.3 42.6 collective-permute-done
  133.0 17.9 maximum_select_fusion.7
  155.2 10.5 dynamic-update-slice.4
  165.8 8.1 reshape.594
  174.0 61.5 collective-permute-done.1
  235.5 12.5 maximum_select_fusion.3
  250.9 18.7 all-gather.1
  278.4 448.3 %all-reduce.22 = (bf16[6400]{0:T(1024)(128)(2,1)S(1)}, bf16[6400]{0:T(1024)(128)(2,1)S(1)}) all-reduce(bf16[6400]{0:T(1024)(128)(2,1)S(1)} %dynamic-update-slice.3, bf16[6400]{0:T(1024)(128)(2,1)S(1)} %dynamic-update-slice.1), channel_id=1, replica_groups=mesh['dp'=8,'seq'=4] {'dp'}, use_global_device_ids=true, to_apply=%add.3 | all-reduce | flops 12800 | bytes 51200
  742.6 7.3 concatenate.63
  749.8 10.0 maximum_select_fusion.2
  759.9 13.4 concatenate.68
  773.2 17.4 fusion.56
  797.1 7.4 broadcast.250
  804.5 39.9 dynamic-update-slice.5
  844.5 17.8 reduce.27
  868.1 31.8 reduce.26
  899.9 12.4 reshape.643
  912.3 9.5 reshape.556
  923.5 7.1 copy.32
  937.7 80.0 %while.28 = (s32[]{:T(128)}, bf16[25,1,256,64]{2,3,1,0:T(8,128)(2,1)S(1)}, f32[25,1,256]{2,1,0:T(1,128)S(1)}, bf16[25,1,256,64]{3,2,1,0:T(8,128)(2,1)}, bf16[25,...) while((s32[]{:T(128)}, ...), condition=%wide.region_5.6_spmd.clone, body=%wide.region_2.5_spmd.clone.sunk | while | flops 69730048 | bytes 3815529 | solution.py:155
  1023.2 447.7 %all-reduce.31.cloned.1.call-done = bf16[10246400]{0:T(1024)(128)(2,1)} async-done(((bf16[10246400]{0:T(1024)(128)(2,1)}), bf16[10246400]{0:T(1024)(128)(2,1)}) %all-reduce.31.cloned.1.call-update) | async-done | bytes 20492816
  1470.9 17.1 slice.87
  1488.0 35.3 slice.74
  1524.0 12.4 convolution_add_fusion
  1536.4 327.7 %all-gather.17.cloned.1.call-done = bf16[10240000]{0:T(1024)(128)(2,1)} async-done(((bf16[1280000]{0:T(1024)(128)(2,1)}), bf16[10240000]{0:T(1024)(128)(2,1)}) %all-gather.17.cloned.1.call-update) | async-done | bytes 20480016 | tf_op jit(solution)/shard_map/all_gather | solution.py:122
  1864.2 33.9 reshape.558
  1898.1 14.1 convert_reduce_fusion
  1912.2 13.4 fusion.82
  1933.7 200.9 %while.29 = (s32[]{:T(128)}, bf16[25,1,256,64]{2,3,1,0:T(8,128)(2,1)S(1)}, f32[25,1,1024,64]{2,3,1,0:T(8,128)}, f32[25,1,1024,64]{2,3,1,0:T(8,128)}, bf16[25,1,2...) while((s32[]{:T(128)}, ...), condition=%wide.region_12.13_spmd.clone, body=%wide.region_10.12_spmd.clone.sunk | while | flops 171179776 | bytes 9515137 | solution.py:232
  2135.2 22.7 fusion.92
  2157.9 48.4 reshape.569
  2206.3 7.1 fusion.89
  2213.4 13.5 reshape.567
  2226.9 18.4 fusion.110
  2245.3 28.0 pad_maximum_fusion
  2273.3 39.9 reshape.568
  2316.9 12.9 fusion.85
  2329.9 36.6 reshape.566
  2369.3 3608.9 %all-reduce.33.cloned.1.call-done = (f32[7680000]{0:T(1024)}, f32[2560000]{0:T(1024)}, f32[10246400]{0:T(1024)}, f32[10240000]{0:T(1024)}) async-done(((f32[7680000]{0:T(1024)}, f32[2560000]{0:T(1024)}, f32[10246400]{0:T(1024)}, f32[10240000]{0:T(1024)}), (f32[7680000]{0:T(1024)}, f32[2560000]{0:T(1024)}, f32[10246400]{0:T(1024)}, f32[10240000]{0:T(1024)})) %all-reduce.33.cloned.1.call-update) | async-done | bytes 122905616
  5999.2 564.3 %all-gather.25.cloned.1.call-done = bf16[8,1,960000]{2,1,0:T(2,128)(2,1)} async-done(((bf16[1,1,960000]{2,1,0:T(2,128)(2,1)}), bf16[8,1,960000]{2,1,0:T(2,128)(2,1)}) %all-gather.25.cloned.1.call-update) | async-done | bytes 15360016 | tf_op jit(solution)/shard_map/all_gather | solution.py:187
  6563.5 325.4 %reduce.28 = bf16[8,960000]{1,0:T(8,128)(2,1)} reduce(bf16[8,1,960000]{2,1,0:T(2,128)(2,1)} %all-gather.25.cloned.1.call-done, bf16[]{:T(256)} %constant.183), dimensions={1}, to_apply=%all-gather.4.reduce_sub_computation | reduce | bytes 30720002 | tf_op jit(solution)/shard_map/all_gather | solution.py:187
  6888.8 33.8 reshape.645
  6922.7 25.2 reshape.565
  6950.1 17.5 fusion.68
  6967.6 8.1 fusion.79
  6977.1 36.4 all-reduce.18
  (489 shorter events, 400.0 us)
Async XLA Ops:
  7.2 41.6 all-gather.19.cloned.1.call-start
  13.4 783.7 %all-reduce.29.cloned.1.call-start = ((), (), s32[]{:S(2)}) async-start(), calls=%async_computation.7 | async-start | bytes 5124096
  88.7 66.5 copy-start.4
  88.8 63.6 copy-start.35
  88.8 63.6 copy-start.36
  88.8 44.2 collective-permute-start
  90.3 64.9 copy-start.14
  150.9 15.0 copy-start.15
  150.9 84.6 %collective-permute-start.1 = (bf16[1920000]{0:T(1024)(128)(2,1)}, bf16[1920000]{0:T(1024)(128)(2,1)}, u32[]{:S(2)}, u32[]{:S(2)}) collective-permute-start(bf16[1920000]{0:T(1024)(128)(2,1)} %maximum_select_fusion.7), channel_id=1, source_target_pairs={{0,8},{4,12},{8,0},{12,4},{16,24},{20,28},{24,16},{28,20},{1,9},{5... | collective-permute-start | bytes 11520008 | tf_op jit(solution)/shard_map/ppermute | solution.py:24
  165.8 678.7 %all-gather.23.cloned.1.call-start = ((), (), s32[]{:S(2)}) async-start(), calls=%async_computation.11 | async-start | bytes 6400000 | tf_op jit(solution)/shard_map/all_gather | solution.py:114
  173.9 694.1 %all-gather.21.cloned.1.call-start = ((), (), s32[]{:S(2)}) async-start(), calls=%async_computation.10 | async-start | bytes 11520000 | tf_op jit(solution)/shard_map/all_gather | solution.py:120
  174.0 76.8 %copy-start.18 = (bf16[80000]{0:T(1024)(128)(2,1)S(1)}, bf16[80000]{0:T(1024)(128)(2,1)}, u32[]{:S(2)}) copy-start(bf16[80000]{0:T(1024)(128)(2,1)} %param.17) | copy-start | bytes 480004
  174.0 97.1 %copy-start.37 = (bf16[200]{0:T(256)(128)(2,1)S(1)}, bf16[200]{0:T(256)(128)(2,1)}, u32[]{:S(2)}) copy-start(bf16[200]{0:T(256)(128)(2,1)} %param.21) | copy-start | bytes 1204
  174.0 97.3 %copy-start.38 = (bf16[200]{0:T(256)(128)(2,1)S(1)}, bf16[200]{0:T(256)(128)(2,1)}, u32[]{:S(2)}) copy-start(bf16[200]{0:T(256)(128)(2,1)} %param.20) | copy-start | bytes 1204
  248.0 478.7 %copy-start.2 = (bf16[1,256,1600]{1,2,0:T(8,128)(2,1)S(1)}, bf16[1,256,1600]{1,2,0:T(8,128)(2,1)}, u32[]{:S(2)}) copy-start(bf16[1,256,1600]{1,2,0:T(8,128)(2,1)} %param.13) | copy-start | bytes 2457604
  248.0 511.9 %collective-permute-start.2 = (bf16[3840000]{0:T(1024)(128)(2,1)}, bf16[3840000]{0:T(1024)(128)(2,1)}, u32[]{:S(2)}, u32[]{:S(2)}) collective-permute-start(bf16[3840000]{0:T(1024)(128)(2,1)} %maximum_select_fusion.3), channel_id=1, source_target_pairs={{0,16},{4,20},{8,24},{12,28},{16,0},{20,4},{24,8},{28,12},{1,17},{... | collective-permute-start | bytes 23040008 | tf_op jit(solution)/shard_map/ppermute | solution.py:24
  269.7 653.8 %all-gather.13.cloned.1.call-start = ((), (), s32[]{:S(2)}) async-start(), calls=%async_computation.2 | async-start | bytes 4096000 | tf_op jit(solution)/shard_map/all_gather | solution.py:149
  727.0 46.3 copy-start.21
  727.3 46.0 copy-start.23
  728.5 44.7 copy-start.16
  728.5 44.7 copy-start.19
  793.0 137.6 %all-gather.15.cloned.1.call-start = ((), (), s32[]{:S(2)}) async-start(), calls=%async_computation.3 | async-start | bytes 4096000 | tf_op jit(solution)/shard_map/all_gather | solution.py:150
  796.4 674.5 %all-reduce.31.cloned.1.call-start = ((), (), s32[]{:S(2)}) async-start(), calls=%async_computation.8 | async-start | bytes 40988672
  844.4 1019.8 %all-gather.17.cloned.1.call-start = ((), (), s32[]{:S(2)}) async-start(), calls=%async_computation.4 | async-start | bytes 23040000 | tf_op jit(solution)/shard_map/all_gather | solution.py:122
  867.2 1446.0 %reduce-scatter.3.cloned.1.call-start = ((), (), s32[]{:S(2)}) async-start(), calls=%async_computation.5 | async-start | bytes 8192000 | tf_op jit(solution)/shard_map/reduce_scatter | solution.py:237
  868.0 1267.2 %copy-start.33 = (bf16[256]{0:T(256)(128)(2,1)}, bf16[256]{0:T(256)(128)(2,1)S(1)}, u32[]{:S(2)}) copy-start(bf16[256]{0:T(256)(128)(2,1)S(1)} %compare_convert_fusion) | copy-start | bytes 1540
  1017.7 5.2 copy-start.9
  1022.9 1204.0 %copy-start = (f32[1,256,1600]{1,2,0:T(8,128)}, f32[1,256,1600]{1,2,0:T(8,128)S(1)}, u32[]{:S(2)}) copy-start(f32[1,256,1600]{1,2,0:T(8,128)S(1)} %get-tuple-element.235) | copy-start | bytes 4915204
  1536.4 361.7 %copy-start.6 = (bf16[1,256,1600]{1,2,0:T(8,128)(2,1)S(1)}, bf16[1,256,1600]{1,2,0:T(8,128)(2,1)}, u32[]{:S(2)}) copy-start(bf16[1,256,1600]{1,2,0:T(8,128)(2,1)} %param.14) | copy-start | bytes 2457604
  1926.1 5.7 copy-start.5
  1926.1 5.7 copy-start.27
  1927.4 4.5 copy-start.13
  2134.6 180.3 %reduce-scatter.5.cloned.1.call-start = ((), (), s32[]{:S(2)}) async-start(), calls=%async_computation.6 | async-start | bytes 8192000 | tf_op jit(solution)/shard_map/reduce_scatter | solution.py:238
  2135.2 3843.0 %all-reduce.33.cloned.1.call-start = ((), (), s32[]{:S(2)}) async-start(), calls=%async_computation.13 | async-start | bytes 245817344
  2157.9 48.4 copy-start.10
  2314.8 15.0 copy-start.11
  2316.9 13.0 copy-start.12
  2366.4 4197.0 %all-gather.25.cloned.1.call-start = ((), (), s32[]{:S(2)}) async-start(), calls=%async_computation.12 | async-start | bytes 34560000 | tf_op jit(solution)/shard_map/all_gather | solution.py:187
  2367.0 4657.0 %all-reduce.35.cloned.1.call-start = ((), (), s32[]{:S(2)}) async-start(), calls=%async_computation.14 | async-start | bytes 30736384
  6922.6 27.3 copy-start.25
  6922.6 27.3 copy-start.26
  6922.6 27.3 copy-start.32
  6922.7 27.4 copy-start.1
  6922.7 27.4 copy-start.31
  6967.6 8.5 copy-start.30
  6975.8 44.9 copy-start.7
  6975.8 44.9 copy-start.28
  6975.8 44.9 copy-start.34
  (7 other events, 20.9 us)
Sparse Core Ops, SparseCore 0:
  13.6 35.1 all-gather.18
  165.9 58.3 all-reduce.28
  226.5 46.5 all-gather.22
  275.4 334.5 all-gather.20
  793.1 27.7 all-gather.12
  823.0 29.7 all-gather.14
  857.4 613.4 all-reduce.30
  1472.5 391.6 all-gather.16
  2134.7 60.0 reduce-scatter.2
  2197.2 60.0 reduce-scatter.4
  2366.5 3611.5 all-reduce.32
  5979.6 583.8 all-gather.24
  6566.8 267.0 all-reduce.34
